TPU v7x, 256 devices: a whole 4x4x8 slice. The times are simulated.
256 devices in a mesh: dm: 4 (over y), freq: 64 (over z, x, core).
Axes of the slice: x: 4, y: 4, z: 8, core: 2. Of those that a mesh axis runs over, the one named last changes fastest.
Arguments:
- series: float32 [16777216], P(('dm', 'freq')), parts along dimension 0, may hold values from -6 to 6
- kernels: float32 [2, 16, 129], replicated, may hold values from -0.5 to 0.5
- half_widths: int32 [16], replicated, may hold values from 32 to 64, as said below
- sub_rows: int32 [3, 16], replicated, may hold values from 0 to 15
Outputs:
- summed: float32 [16, 8388608], P(None, ('dm', 'freq')), parts along dimension 1
There are 4 independent parts, one for each index of `dm`. A program takes and returns all parts, laid end to end along the dimension named above; an argument that names none is the same for every part. Nothing has to cross between parts.
Inputs may be any that keep to these rules, and one draw needn't show every extreme that they name: Template t's kernel is nonzero only at offsets |j| <= half_widths[t]; some template has half-width exactly 64.
All inputs are finite; a program needn't handle non-finite values.
Results may differ from a plain program's by a relative error of at most 0.000051.
Values sent between devices are 32-bit elements; how exact they have to be, the bound alone decides.
No kernel may reach another device: no remote copies, remote signals or barrier semaphores. Data moves between devices by JAX's collectives and lax.ppermute only.
A program may use at most 128 MiB of HBM per device.

v0:
```python
import math

import jax
import jax.numpy as jnp
import numpy as np
from jax import lax
from jax.experimental import pallas as pl
from jax.experimental.pallas import tpu as pltpu
from jax.sharding import PartitionSpec as P

SAMPLES = 4194304
TEMPL = 16
MAXHALF = 64
MEMBERS = 64
LANES = 128
ROWS_OUT = 21

highest = lax.Precision.HIGHEST
f32 = jnp.float32
bf16 = jnp.bfloat16

MAIN, HALF2, HALF3, HALF1 = 0, 1, 2, 3
COUNTS = (256, 128, 192, 64)
BASES = (0, 264, 400, 600)
GATHERED = 672
WINDOWS = 640


def unit(product, length):
    angles = np.asarray(product, np.float64) % length * (-2.0 * math.pi / length)
    return np.cos(angles), np.sin(angles)


def first_matrix():
    matrix = np.zeros((128, 128))
    wide = np.arange(128)
    for k0 in range(64):
        real, imag = unit(k0 * wide, 128)
        matrix[2 * k0] = real
        matrix[2 * k0 + 1] = imag
    matrix[1] = unit(64 * wide, 128)[0]
    return matrix.astype(np.float32)


def row_order():
    at = np.arange(256)
    return 4 * (at % 64) + at // 64


def second_matrix():
    q, a = np.arange(256)[:, None], row_order()[None, :]
    real, imag = unit(q * a, 256)
    return np.block([[real, -imag], [imag, real]]).astype(np.float32)


def middle_twiddle():
    q, b = np.arange(256)[:, None], np.arange(128)[None, :]
    real, imag = unit(q * b, 32768)
    return np.stack([real, imag]).astype(np.float32)


def third_matrix():
    c, b = np.arange(72)[:, None], np.arange(128)[None, :]
    real, imag = unit(c * b, 128)
    norm = 1.0 / math.sqrt(SAMPLES)
    return (np.block([[real, -imag], [imag, real]]) * norm).astype(np.float32)


def spread_matrices():
    lane, s = np.arange(128)[:, None], np.arange(128)[None, :]
    one = np.concatenate([lane == 32 * u + s // 4 for u in range(4)], axis=1)
    two = np.concatenate([lane == 64 * u + s // 2 for u in range(2)], axis=1)
    threes = [
        np.concatenate(
            [128 * v + lane == 96 * beta + 3 * s // 4 for beta in (v, v + 1)], axis=1
        )
        for v in range(3)
    ]
    one, two, threes = (np.concatenate([m, m], axis=-2) for m in (one, two, np.stack(threes)))
    return one.astype(bf16), two.astype(bf16), threes.astype(bf16)


def flip_matrix():
    at = np.arange(64)
    return ((64 - at[:, None]) % 64 == at[None, :]).astype(bf16)


def halves(values):
    high = values.astype(bf16)
    return high, (values - high.astype(f32)).astype(bf16)


def first_kernel(matrix_ref, x_ref, out_ref):
    for jj in range(4):
        block = x_ref[pl.ds(jj, 128, stride=4), :]
        out_ref[pl.ds(jj, 128, stride=4), :] = jnp.dot(
            matrix_ref[...], block, precision=highest, preferred_element_type=f32
        )


def spectrum_kernel(
    x_ref, turns_ref, second_ref, middle_ref, third_ref, flag_ref, out_ref, lines_ref, wins_ref
):
    real = jnp.concatenate([x_ref[pl.ds(jj, 64, stride=8), :] for jj in range(4)], axis=0)
    imag = jnp.concatenate([x_ref[pl.ds(4 + jj, 64, stride=8), :] for jj in range(4)], axis=0)
    special = flag_ref[0] == 0
    lone = jnp.where(special, imag, real)
    kept = jnp.where(special, jnp.zeros_like(imag), imag)
    at, bt, ct, dt = turns_ref[0], turns_ref[1], turns_ref[2], turns_ref[3]
    stacked = jnp.concatenate(
        [
            jnp.concatenate([real * at - kept * bt, lone * ct - kept * dt], axis=1),
            jnp.concatenate([real * bt + kept * at, -(lone * dt + kept * ct)], axis=1),
        ],
        axis=0,
    )
    stage = jnp.dot(second_ref[...], stacked, precision=highest, preferred_element_type=f32)
    mid_real, mid_imag = middle_ref[0], middle_ref[1]
    for half in range(2):
        part = stage[:, half * 128 : half * 128 + 128]
        part_real, part_imag = part[:256], part[256:]
        turned = jnp.concatenate(
            [
                part_real * mid_real - part_imag * mid_imag,
                part_real * mid_imag + part_imag * mid_real,
            ],
            axis=1,
        )
        lines = lax.dot_general(
            third_ref[...],
            turned,
            (((1,), (1,)), ((), ())),
            precision=highest,
            preferred_element_type=f32,
        )
        c_at = lax.broadcasted_iota(jnp.int32, (72, 256), 0)
        q_at = lax.broadcasted_iota(jnp.int32, (72, 256), 1)
        outside = jnp.logical_and(q_at == 0, c_at == (0 if half else 64))
        for ri in range(2):
            arr = half * 2 + ri
            kept_lines = jnp.where(outside, 0.0, lines[ri * 72 : ri * 72 + 72])
            for tile in range(2):
                lines_ref[arr, tile] = kept_lines[:, tile * 128 : tile * 128 + 128]
    low = lax.broadcasted_iota(jnp.int32, (16, 128), 1) < 64

    def swap(tile):
        return pltpu.roll(tile, 64, 1)

    for arr in range(4):
        for u in range(2):
            wins_ref[arr, u] = lines_ref[arr, u]
            wins_ref[arr, 2, pl.ds(u, 32, stride=2), :] = lines_ref[arr, u, 0:32, :]
        wins_ref[arr, 2, 64:65, :] = lines_ref[arr, 0, 32:33, :]
        t = [
            [lines_ref[arr, w, pl.ds(v, 16, stride=3), :] for w in range(2)]
            for v in range(3)
        ]
        firsts = (
            t[0][0],
            jnp.where(low, swap(t[0][1]), swap(t[1][0])),
            t[1][1],
            jnp.where(low, swap(t[2][0]), swap(t[2][1])),
        )
        seconds = (t[0][1], swap(t[1][0]), t[2][0], swap(t[2][1]))
        s0 = lines_ref[arr, 0, 0:16, :]
        s1 = lines_ref[arr, 1, 0:16, :]
        quarters = (swap(s0), s0, swap(s1), s1)
        for w in range(4):
            wins_ref[arr, 3, pl.ds(w, 16, stride=4), :] = firsts[w]
            wins_ref[arr, 4, pl.ds(w, 16, stride=4), :] = jnp.where(low, seconds[w], quarters[w])
        wins_ref[arr, 3, 64:65, :] = lines_ref[arr, 0, 48:49, :]
        wins_ref[arr, 4, 64:65, :] = pltpu.roll(lines_ref[arr, 0, 16:17, :], 64, 1)
    lane = lax.broadcasted_iota(jnp.int32, (64, 128), 1)
    tails = jnp.zeros((64, 128), f32)
    for arr in range(4):
        for tile in range(5):
            row = arr * 5 + tile
            out_ref[pl.ds(row, 64, stride=ROWS_OUT), :] = wins_ref[arr, tile, 0:64, :]
        for g, (tile, column) in enumerate(((0, 0), (2, 0), (3, 0), (4, 64))):
            value = wins_ref[arr, tile, 1:65, column : column + 1]
            tails = jnp.where(lane == arr * 4 + g, value, tails)
    out_ref[pl.ds(20, 64, stride=ROWS_OUT), :] = tails


def taps_kernel(v_ref, flip_ref, high_ref, low_ref):
    natural = [
        pltpu.roll(
            jnp.broadcast_to(v_ref[part, 0], (256, 256)), 0, 1, stride=1, stride_axis=0
        )[:, :128]
        for part in range(2)
    ]
    for lower in range(2):
        pair = [-natural[1], natural[0]] if lower else natural
        splits = halves(jnp.concatenate(pair, axis=1))
        for target, split in zip((high_ref, low_ref), splits):
            for at in range(2):
                base = lower * 256 + at * 128
                target[0, base : base + 64] = jnp.dot(
                    flip_ref[...],
                    split[at * 128 : at * 128 + 64],
                    preferred_element_type=f32,
                ).astype(bf16)
                target[0, base + 64 : base + 128] = split[at * 128 + 64 : at * 128 + 128]


def power_kernel(
    rows_ref,
    x_ref,
    high_ref,
    low_ref,
    one_ref,
    two_ref,
    three_ref,
    out_ref,
    gathered_ref,
    win_high_ref,
    win_low_ref,
    sum_ref,
    lower_ref,
):
    step = pl.program_id(0)

    @pl.when(step == 0)
    def _():
        tails = x_ref[pl.ds(20, 64, stride=ROWS_OUT), :]
        tails = jnp.transpose(jnp.concatenate([tails, tails], axis=0))
        lane = lax.broadcasted_iota(jnp.int32, (1, 128), 1)
        for ri in range(2):
            for tile in range(5):
                block = jnp.concatenate(
                    [
                        x_ref[pl.ds((half * 2 + ri) * 5 + tile, 64, stride=ROWS_OUT), :]
                        for half in (1, 0)
                    ],
                    axis=0,
                )
                block = jnp.transpose(block)
                if tile < 2:
                    gathered_ref[ri, tile * 128 : tile * 128 + 128] = block
                elif tile == 2:
                    gathered_ref[ri, BASES[1] : BASES[1] + 128] = block
                elif tile == 3:
                    gathered_ref[ri, BASES[2] : BASES[2] + 128] = block
                else:
                    gathered_ref[ri, BASES[2] + 128 : BASES[2] + 192] = block[:64]
                    gathered_ref[ri, BASES[3] : BASES[3] + 64] = block[64:]
            for g in range(4):
                upper = tails[(2 + ri) * 4 + g : (2 + ri) * 4 + g + 1]
                lower = tails[ri * 4 + g : ri * 4 + g + 1]
                at = BASES[g] + COUNTS[g]
                gathered_ref[ri, at : at + 1] = jnp.where(lane < 64, upper, lower)
        places = [(beta * 64, beta, 4) for beta in range(4)]
        places += [(256 + v * 64, BASES[1] + v, 2) for v in range(2)]
        places += [(384 + v * 64, BASES[2] + v, 3) for v in range(3)]
        places += [(576, BASES[3], 1)]
        for target, source, stride in places:
            for ri in range(2):
                for shift in range(2):
                    at = source + shift
                    block = gathered_ref[ri, pl.ds(at, 64, stride=stride), :]
                    span = slice((ri * 2 + shift) * 128, (ri * 2 + shift) * 128 + 128)
                    high, low = halves(block)
                    win_high_ref[target : target + 64, span] = high
                    win_low_ref[target : target + 64, span] = low

    response = jnp.dot(win_high_ref[...], high_ref[0], preferred_element_type=f32)
    response += jnp.dot(win_low_ref[...], high_ref[0], preferred_element_type=f32)
    response += jnp.dot(win_high_ref[...], low_ref[0], preferred_element_type=f32)
    real, imag = response[:, :128], response[:, 128:]
    power = real * real + imag * imag
    sum_ref[pl.ds(step * 256, 256), :] = power[:256]
    high, low = halves(power[256:])
    lower_ref[step, :, 0:128] = high
    lower_ref[step, :, 128:256] = low

    @pl.when(step == TEMPL - 1)
    def _():
        for t in range(TEMPL):
            r1, r2, r3 = rows_ref[0, t], rows_ref[1, t], rows_ref[2, t]
            single = jnp.dot(lower_ref[r1, 320:384], one_ref[...], preferred_element_type=f32)
            double = jnp.dot(lower_ref[r2, 0:128], two_ref[...], preferred_element_type=f32)
            triple = [
                jnp.dot(
                    lower_ref[r3, 128 + 64 * v : 192 + 64 * v],
                    three_ref[v],
                    preferred_element_type=f32,
                )
                for v in range(3)
            ]
            thirds = (
                triple[0][:, :128],
                triple[0][:, 128:] + triple[1][:, :128],
                triple[1][:, 128:] + triple[2][:, :128],
                triple[2][:, 128:],
            )
            for beta in range(4):
                v, u = beta // 2, beta % 2
                at = t * 256 + beta * 64
                sum_ref[at : at + 64, :] = (
                    sum_ref[at : at + 64, :]
                    + single[:, beta * 128 : beta * 128 + 128]
                    + double[v * 64 : v * 64 + 64, u * 128 : u * 128 + 128]
                    + thirds[beta]
                )
        for beta in range(4):
            for i in range(64):
                b = 4 * i + beta
                for t in range(0, TEMPL, 8):
                    out_ref[t : t + 8, b * 128 : b * 128 + 128] = sum_ref[
                        pl.ds(t * 256 + beta * 64 + i, 8, stride=256), :
                    ]


def swap_blocks(values):
    return lax.all_to_all(values, "freq", split_axis=0, concat_axis=0, tiled=True)


def turn_tables(position):
    m = 128 * jnp.asarray(row_order(), jnp.int32)[:, None] + jnp.arange(128, dtype=jnp.int32)
    tables = []
    for residue in (position, jnp.where(position == 0, 64, position)):
        angles = (m * residue).astype(f32) * (-2.0 * math.pi / SAMPLES)
        tables += [jnp.cos(angles), jnp.sin(angles)]
    return jnp.stack(tables)


def tap_rows(kernels, half_widths):
    offsets = jnp.abs(jnp.arange(2 * MAXHALF + 1, dtype=jnp.int32) - MAXHALF)
    inside = offsets[None, :] <= half_widths[:, None]
    taps = jnp.where(inside[None], kernels, 0.0)
    return jnp.concatenate(
        [taps[:, :, 0:1], jnp.zeros((2, TEMPL, 127), f32), taps[:, :, :0:-1]], axis=2
    ).reshape(2, TEMPL, 1, 256)


def whole(shape):
    return pl.BlockSpec(shape, lambda i: (0,) * len(shape))


def on_device(series, kernels, half_widths, sub_rows):
    position = lax.axis_index("freq")
    blocks = series.reshape(2, MEMBERS, 4, LANES).transpose(1, 0, 2, 3).reshape(512, LANES)
    arrived = swap_blocks(blocks)
    streams = pl.pallas_call(
        first_kernel, out_shape=jax.ShapeDtypeStruct((512, LANES), f32), name="first"
    )(jnp.asarray(first_matrix()), arrived)
    arrived = swap_blocks(streams)
    outgoing = pl.pallas_call(
        spectrum_kernel,
        in_specs=[pl.BlockSpec()] * 5 + [pl.BlockSpec(memory_space=pltpu.SMEM)],
        out_shape=jax.ShapeDtypeStruct((MEMBERS * ROWS_OUT, LANES), f32),
        scratch_shapes=[pltpu.VMEM((4, 2, 72, 128), f32), pltpu.VMEM((4, 5, 72, 128), f32)],
        name="spectrum",
    )(
        arrived,
        turn_tables(position),
        jnp.asarray(second_matrix()),
        jnp.asarray(middle_twiddle()),
        jnp.asarray(third_matrix()),
        position.reshape(1),
    )
    arrived = swap_blocks(outgoing)
    matrix = jax.ShapeDtypeStruct((TEMPL, 512, 256), bf16)
    one_block = pl.BlockSpec((1, 512, 256), lambda i: (i, 0, 0))
    tap_high, tap_low = pl.pallas_call(
        taps_kernel,
        grid=(TEMPL,),
        in_specs=[pl.BlockSpec((2, 1, 1, 256), lambda i: (0, i, 0, 0)), whole((64, 64))],
        out_specs=[one_block, one_block],
        out_shape=[matrix, matrix],
        name="taps",
    )(tap_rows(kernels, half_widths), jnp.asarray(flip_matrix()))
    one, two, threes = (jnp.asarray(m) for m in spread_matrices())
    return pl.pallas_call(
        power_kernel,
        grid=(TEMPL,),
        in_specs=[
            pl.BlockSpec(memory_space=pltpu.SMEM),
            whole((MEMBERS * ROWS_OUT, LANES)),
            one_block,
            one_block,
            whole((256, 512)),
            whole((256, 256)),
            whole((3, 256, 256)),
        ],
        out_specs=whole((TEMPL, 256 * LANES)),
        out_shape=jax.ShapeDtypeStruct((TEMPL, 256 * LANES), f32),
        scratch_shapes=[
            pltpu.VMEM((2, GATHERED, 128), f32),
            pltpu.VMEM((WINDOWS, 512), bf16),
            pltpu.VMEM((WINDOWS, 512), bf16),
            pltpu.VMEM((TEMPL * 256, 128), f32),
            pltpu.VMEM((TEMPL, 384, 256), bf16),
        ],
        name="power",
    )(sub_rows, arrived, tap_high, tap_low, one, two, threes)


def solution(mesh):
    in_specs = (P(("dm", "freq")), P(), P(), P())
    out_specs = P(None, ("dm", "freq"))
    return jax.shard_map(
        on_device, mesh=mesh, in_specs=in_specs, out_specs=out_specs, check_vma=False
    )
```

profile of v0, /device:TPU:1, one launch (start us, length us, event | category | flops | bytes accessed | tf_op | source)
XLA Modules:
  0.0 104.5 jit_solution(9994701605125854625)
XLA Ops:
  0.0 1.0 copy.16
  1.0 0.2 copy.17
  1.1 26.0 %all_to_all.33 = f32[64,8,128]{2,1,0:T(8,128)} all-to-all(f32[64,8,128]{2,1,0:T(8,128)S(1)} %copy.17), channel_id=1, replica_groups=mesh['dm'=4,'freq'=64] {'freq'}, dimensions={0} | all-to-all | bytes 524288 | tf_op jit(solution)/shard_map/all_to_all | solution.py:315
  27.1 2.0 %first.1 = f32[512,128]{1,0:T(8,128)} custom-call(f32[128,128]{1,0:T(8,128)} %constant.36.clone.matrix_ref, f32[512,128]{1,0:T(8,128)} %bitcast.10), custom_call_target="tpu_custom_call" | custom-call | tf_op jit(solution)/shard_map/first/pallas_call | solution.py:344
  29.1 0.0 copy-start.2
  29.1 0.0 copy-start.1
  29.1 4.9 %all-to-all-start.1 = ((f32[64,8,128]{2,1,0:T(8,128)}), f32[64,8,128]{2,1,0:T(8,128)S(1)}, u32[]{:S(2)}, u32[]{:S(2)}) async-start(f32[64,8,128]{2,1,0:T(8,128)} %bitcast.9), calls=%async_computation.1 | async-start | bytes 524288 | tf_op jit(solution)/shard_map/all_to_all | solution.py:315
  34.1 1.7 %fusion.1 = (f32[1,256,128]{2,1,0:T(8,128)S(1)}, f32[1,256,128]{2,1,0:T(8,128)S(1)}, f32[1,256,128]{2,1,0:T(8,128)S(1)}, f32[1,256,128]{2,1,0:T(8,128)S(1)}) fusion(s32[]{:T(128)} %axis_index.12, s32[256]{0:T(256)} %constant.45, s32[]{:T(128)S(6)} %select_n.8), kind=kLoop, calls=%fused_computation.5 | loop fusion | flops 229376 | bytes 525320 | tf_op jit(solution)/shard_map/cos | solution.py:323
  35.8 0.8 pad_maximum_fusion.turns_ref
  36.6 10.5 %all-to-all-done.1 = f32[64,8,128]{2,1,0:T(8,128)S(1)} async-done(((f32[64,8,128]{2,1,0:T(8,128)}), f32[64,8,128]{2,1,0:T(8,128)S(1)}, u32[]{:S(2)}, u32[]{:S(2)}) %all-to-all-start.1) | async-done | bytes 262176 | tf_op jit(solution)/shard_map/all_to_all | solution.py:315
  47.1 0.0 copy-start
  47.1 0.7 copy-done
  47.8 5.0 %spectrum.1 = f32[1344,128]{1,0:T(8,128)} custom-call(f32[512,128]{1,0:T(8,128)} %bitcast.8, f32[4,256,128]{2,1,0:T(8,128)} %pad_maximum_fusion.turns_ref, f32[512,512]{1,0:T(8,128)} %constant.38.clone.second_ref, f32[2,256,128]{2,1,0:T(8,128)} %constant.39.clone.middle_ref, f32[144,256]{1,0:T(8,128)} %constant.40.clone.third_ref, s32[1]{0:T(128)} %bitcast.6.flag_ref), custom_call_target="tpu_custom_call" | custom-call | tf_op jit(solution)/shard_map/spectrum/pallas_call | solution.py:348
  52.8 2.0 %all_to_all.27 = f32[64,21,128]{2,1,0:T(8,128)} reshape(f32[1344,128]{1,0:T(8,128)} %spectrum.1) | data formatting | bytes 1376256 | tf_op jit(solution)/shard_map/all_to_all | solution.py:315
  54.9 4.8 %all-to-all-start.2 = ((f32[64,21,128]{2,1,0:T(8,128)}), f32[64,21,128]{2,1,0:T(8,128)S(1)}, u32[]{:S(2)}, u32[]{:S(2)}) async-start(f32[64,21,128]{2,1,0:T(8,128)} %all_to_all.27), calls=%async_computation.2 | async-start | bytes 1572864 | tf_op jit(solution)/shard_map/all_to_all | solution.py:315
  59.7 0.0 copy-done.2
  59.7 0.1 broadcast_compare_fusion
  59.7 0.0 copy-done.1
  59.8 0.1 slice.9
  59.8 0.1 rev.3
  59.9 0.1 pad.1.clone
  60.0 0.6 reshape.169.v_ref
  60.6 10.6 %taps.1 = (bf16[16,512,256]{2,1,0:T(8,128)(2,1)}, bf16[16,512,256]{2,1,0:T(8,128)(2,1)}) custom-call(f32[2,16,1,256]{3,2,1,0:T(1,128)} %reshape.169.v_ref, bf16[64,64]{1,0:T(8,128)(2,1)} %constant.41.clone.flip_ref), custom_call_target="tpu_custom_call" | custom-call | tf_op jit(solution)/shard_map/taps/pallas_call | solution.py:365
  71.2 11.5 %all-to-all-done.2 = f32[64,21,128]{2,1,0:T(8,128)S(1)} async-done(((f32[64,21,128]{2,1,0:T(8,128)}), f32[64,21,128]{2,1,0:T(8,128)S(1)}, u32[]{:S(2)}, u32[]{:S(2)}) %all-to-all-start.2) | async-done | bytes 688160 | tf_op jit(solution)/shard_map/all_to_all | solution.py:315
  82.6 0.9 all_to_all.29.x_ref
  83.6 20.9 %power.1 = f32[16,32768]{1,0:T(8,128)} custom-call(s32[3,16]{1,0:T(4,128)} %rows_ref.1, f32[1344,128]{1,0:T(8,128)} %all_to_all.29.x_ref, bf16[16,512,256]{2,1,0:T(8,128)(2,1)} %get-tuple-element.7.high_ref, bf16[16,512,256]{2,1,0:T(8,128)(2,1)} %get-tuple-element.8.low_ref, bf16[256,512]{1,0:T(8,128)(2,1)} %constant.42.clone.one_ref, ...), custom_call_target="tpu_custom_call" | custom-call | tf_op jit(solution)/shard_map/power/pallas_call | solution.py:374
  (5 shorter events, 0.0 us)
Async XLA Ops:
  29.1 30.5 %copy-start.2 = (s32[16]{0:T(128)S(1)}, s32[16]{0:T(128)}, u32[]{:S(2)}) copy-start(s32[16]{0:T(128)} %param.15) | copy-start | bytes 196
  29.1 30.6 %copy-start.1 = (f32[2,16,129]{2,1,0:T(8,128)S(1)}, f32[2,16,129]{2,1,0:T(8,128)}, u32[]{:S(2)}) copy-start(f32[2,16,129]{2,1,0:T(8,128)} %param.14) | copy-start | bytes 49540
  29.1 18.0 %all-to-all-start.1 = ((f32[64,8,128]{2,1,0:T(8,128)}), f32[64,8,128]{2,1,0:T(8,128)S(1)}, u32[]{:S(2)}, u32[]{:S(2)}) async-start(f32[64,8,128]{2,1,0:T(8,128)} %bitcast.9), calls=%async_computation.1 | async-start | bytes 524288 | tf_op jit(solution)/shard_map/all_to_all | solution.py:315
  47.1 0.7 copy-start
  54.9 27.8 %all-to-all-start.2 = ((f32[64,21,128]{2,1,0:T(8,128)}), f32[64,21,128]{2,1,0:T(8,128)S(1)}, u32[]{:S(2)}, u32[]{:S(2)}) async-start(f32[64,21,128]{2,1,0:T(8,128)} %all_to_all.27), calls=%async_computation.2 | async-start | bytes 1572864 | tf_op jit(solution)/shard_map/all_to_all | solution.py:315
where the time goes:
time: 106 us; the launch traced here: 105 us
  Pallas kernels  38.5 us (36%)
  blocking collectives  26 us (25%)
  waiting for transfers between devices  22 us (21%)
  starting transfers between devices  9.68 us (9%)
  local copies, waits for them, and re-layouts  5.67 us (5%)
  other arithmetic  2.61 us (2%)
    all_to_all x1, blocking collectives, swap_blocks(): lax.all_to_all(values, 'freq', split_axis=0, concat_axis=0, tiled=True)  26 us
    all_to_all x2, waiting for transfers between devices, swap_blocks(): lax.all_to_all(values, 'freq', split_axis=0, concat_axis=0, tiled=True)  22 us
    pallas_call x1, Pallas kernels, on_device(): pl.pallas_call(power_kernel, grid=(TEMPL,), in_specs=[pl.BlockSpec(memory...  20.9 us
    pallas_call x1, Pallas kernels, on_device(): pl.pallas_call(taps_kernel, grid=(TEMPL,), in_specs=[pl.BlockSpec((2, 1,...  10.6 us
    all_to_all x2, starting transfers between devices, swap_blocks(): lax.all_to_all(values, 'freq', split_axis=0, concat_axis=0, tiled=True)  9.68 us
    pallas_call x1, Pallas kernels, on_device(): pl.pallas_call(spectrum_kernel, in_specs=[pl.BlockSpec()] * 5 + [pl.Block...  5 us
    all_to_all x3, local copies, waits for them, and re-layouts, swap_blocks(): lax.all_to_all(values, 'freq', split_axis=0, concat_axis=0, tiled=True)  3.14 us
  transfers between devices with their start and end apart: 2, of which 2 were waited for; matrix products, arithmetic and copies ran while one was open for 3% of the time, Pallas kernels for 10%

commit v1 on v0

v1 whole, which is shorter than its diff:
```python
import math

import jax
import jax.numpy as jnp
import numpy as np
from jax import lax
from jax.experimental import pallas as pl
from jax.experimental.pallas import tpu as pltpu
from jax.sharding import PartitionSpec as P

SAMPLES = 4194304
TEMPL = 16
MAXHALF = 64
MEMBERS = 64
LANES = 128
ROWS_OUT = 24

f32 = jnp.float32
bf16 = jnp.bfloat16

MAIN, HALF2, HALF3, HALF1 = 0, 1, 2, 3
COUNTS = (256, 128, 192, 64)
BASES = (0, 264, 400, 600)
GATHERED = 672
WINDOWS = 640
PAIRS = 2
STEPS = TEMPL // 2 // PAIRS


def unit(product, length):
    angles = np.asarray(product, np.float64) % length * (-2.0 * math.pi / length)
    return np.cos(angles), np.sin(angles)


def first_matrix():
    matrix = np.zeros((128, 128))
    wide = np.arange(128)
    for k0 in range(64):
        real, imag = unit(k0 * wide, 128)
        matrix[2 * k0] = real
        matrix[2 * k0 + 1] = imag
    matrix[1] = unit(64 * wide, 128)[0]
    return matrix.astype(np.float32)


def row_order():
    at = np.arange(256)
    return 4 * (at % 64) + at // 64


def second_matrix():
    q, a = np.arange(256)[:, None], row_order()[None, :]
    real, imag = unit(q * a, 256)
    return np.block([[real, -imag], [imag, real]]).astype(np.float32)


def middle_twiddle():
    q, b = np.arange(256)[:, None], np.arange(128)[None, :]
    real, imag = unit(q * b, 32768)
    return np.stack([real, imag]).astype(np.float32)


def third_matrix():
    c, b = np.arange(72)[:, None], np.arange(128)[None, :]
    real, imag = unit(c * b, 128)
    norm = 1.0 / math.sqrt(SAMPLES)
    return (np.block([[real, -imag], [imag, real]]) * norm).astype(np.float32)


def spread_matrices():
    lane, s = np.arange(128)[:, None], np.arange(128)[None, :]
    pairs = []
    for pair in range(2):
        columns = []
        for u in range(2):
            beta = 2 * pair + u
            pieces = [lane == 32 * beta + s // 4, lane == 64 * u + s // 2]
            for v in (pair, pair + 1):
                pieces.append(128 * v + lane == 96 * beta + 3 * s // 4)
            columns.append(np.concatenate([np.concatenate([m, m]) for m in pieces]))
        pairs.append(np.concatenate(columns, axis=1))
    return np.stack(pairs).astype(bf16)


def flip_matrix():
    at = np.arange(64)
    return ((64 - at[:, None]) % 64 == at[None, :]).astype(bf16)


def halves(values):
    high = values.astype(bf16)
    return high, (values - high.astype(f32)).astype(bf16)


def constant_halves(matrix):
    high = matrix.astype(bf16)
    low = (matrix - high.astype(np.float32)).astype(bf16)
    return jnp.asarray(np.stack([high, low]))


def product(left, right, dims=((1,), (0,))):
    (left_at,), (right_at,) = dims
    return lax.dot_general(
        jnp.concatenate([left[0], left[0], left[1]], axis=left_at),
        jnp.concatenate([right[0], right[1], right[0]], axis=right_at),
        (dims, ((), ())),
        preferred_element_type=f32,
    )


def first_kernel(matrix_ref, x_ref, out_ref):
    samples = jnp.concatenate([x_ref[pl.ds(jj, 128, stride=4), :] for jj in range(4)], axis=1)
    streams = product((matrix_ref[0], matrix_ref[1]), halves(samples))
    for jj in range(4):
        out_ref[pl.ds(jj, 128, stride=4), :] = streams[:, jj * 128 : jj * 128 + 128]


def spectrum_kernel(
    x_ref, turns_ref, second_ref, middle_ref, third_ref, flag_ref, out_ref, lines_ref, wins_ref
):
    real = jnp.concatenate([x_ref[pl.ds(jj, 64, stride=8), :] for jj in range(4)], axis=0)
    imag = jnp.concatenate([x_ref[pl.ds(4 + jj, 64, stride=8), :] for jj in range(4)], axis=0)
    special = flag_ref[0] == 0
    lone = jnp.where(special, imag, real)
    kept = jnp.where(special, jnp.zeros_like(imag), imag)
    at, bt, ct, dt = turns_ref[0], turns_ref[1], turns_ref[2], turns_ref[3]
    stacked = jnp.concatenate(
        [
            jnp.concatenate([real * at - kept * bt, lone * ct - kept * dt], axis=1),
            jnp.concatenate([real * bt + kept * at, -(lone * dt + kept * ct)], axis=1),
        ],
        axis=0,
    )
    stage = product((second_ref[0], second_ref[1]), halves(stacked))
    mid_real, mid_imag = middle_ref[0], middle_ref[1]
    for half in range(2):
        part = stage[:, half * 128 : half * 128 + 128]
        part_real, part_imag = part[:256], part[256:]
        turned = jnp.concatenate(
            [
                part_real * mid_real - part_imag * mid_imag,
                part_real * mid_imag + part_imag * mid_real,
            ],
            axis=1,
        )
        lines = product((third_ref[0], third_ref[1]), halves(turned), ((1,), (1,)))
        c_at = lax.broadcasted_iota(jnp.int32, (72, 256), 0)
        q_at = lax.broadcasted_iota(jnp.int32, (72, 256), 1)
        outside = jnp.logical_and(q_at == 0, c_at == (0 if half else 64))
        for ri in range(2):
            arr = half * 2 + ri
            kept_lines = jnp.where(outside, 0.0, lines[ri * 72 : ri * 72 + 72])
            for tile in range(2):
                lines_ref[arr, tile] = kept_lines[:, tile * 128 : tile * 128 + 128]
    low = lax.broadcasted_iota(jnp.int32, (16, 128), 1) < 64

    def swap(tile):
        return pltpu.roll(tile, 64, 1)

    for arr in range(4):
        for u in range(2):
            wins_ref[arr, u] = lines_ref[arr, u]
            wins_ref[arr, 2, pl.ds(u, 32, stride=2), :] = lines_ref[arr, u, 0:32, :]
        wins_ref[arr, 2, 64:65, :] = lines_ref[arr, 0, 32:33, :]
        t = [
            [lines_ref[arr, w, pl.ds(v, 16, stride=3), :] for w in range(2)]
            for v in range(3)
        ]
        firsts = (
            t[0][0],
            jnp.where(low, swap(t[0][1]), swap(t[1][0])),
            t[1][1],
            jnp.where(low, swap(t[2][0]), swap(t[2][1])),
        )
        seconds = (t[0][1], swap(t[1][0]), t[2][0], swap(t[2][1]))
        s0 = lines_ref[arr, 0, 0:16, :]
        s1 = lines_ref[arr, 1, 0:16, :]
        quarters = (swap(s0), s0, swap(s1), s1)
        for w in range(4):
            wins_ref[arr, 3, pl.ds(w, 16, stride=4), :] = firsts[w]
            wins_ref[arr, 4, pl.ds(w, 16, stride=4), :] = jnp.where(low, seconds[w], quarters[w])
        wins_ref[arr, 3, 64:65, :] = lines_ref[arr, 0, 48:49, :]
        wins_ref[arr, 4, 64:65, :] = pltpu.roll(lines_ref[arr, 0, 16:17, :], 64, 1)
    lane = lax.broadcasted_iota(jnp.int32, (64, 128), 1)
    tails = jnp.zeros((64, 128), f32)
    for arr in range(4):
        for tile in range(5):
            row = arr * 5 + tile
            out_ref[pl.ds(row, 64, stride=ROWS_OUT), :] = wins_ref[arr, tile, 0:64, :]
        for g, (tile, column) in enumerate(((0, 0), (2, 0), (3, 0), (4, 64))):
            value = wins_ref[arr, tile, 1:65, column : column + 1]
            tails = jnp.where(lane == arr * 4 + g, value, tails)
    out_ref[pl.ds(20, 64, stride=ROWS_OUT), :] = tails


def taps_kernel(v_ref, flip_ref, high_ref, low_ref):
    natural = [
        jnp.concatenate(
            [
                pltpu.roll(
                    jnp.broadcast_to(v_ref[part, t], (256, 256)), 0, 1, stride=1, stride_axis=0
                )[:, :128]
                for t in range(2)
            ],
            axis=1,
        )
        for part in range(2)
    ]
    trio = (natural[0], natural[1] - natural[0], natural[0] + natural[1])
    for which, matrix in enumerate(trio):
        for target, split in zip((high_ref, low_ref), halves(matrix)):
            for base in (0, 128):
                target[0, which, base : base + 64] = jnp.dot(
                    flip_ref[...], split[base : base + 64], preferred_element_type=f32
                ).astype(bf16)
                target[0, which, base + 64 : base + 128] = split[base + 64 : base + 128]


def gather_windows(x_ref, gathered_ref, win_high_ref, win_low_ref):
    tails = x_ref[pl.ds(20, 64, stride=ROWS_OUT), :]
    tails = jnp.transpose(jnp.concatenate([tails, tails], axis=0))
    lane = lax.broadcasted_iota(jnp.int32, (1, 128), 1)
    for ri in range(2):
        for tile in range(5):
            block = jnp.concatenate(
                [
                    x_ref[pl.ds((half * 2 + ri) * 5 + tile, 64, stride=ROWS_OUT), :]
                    for half in (1, 0)
                ],
                axis=0,
            )
            block = jnp.transpose(block)
            if tile < 2:
                gathered_ref[ri, tile * 128 : tile * 128 + 128] = block
            elif tile == 2:
                gathered_ref[ri, BASES[1] : BASES[1] + 128] = block
            elif tile == 3:
                gathered_ref[ri, BASES[2] : BASES[2] + 128] = block
            else:
                gathered_ref[ri, BASES[2] + 128 : BASES[2] + 192] = block[:64]
                gathered_ref[ri, BASES[3] : BASES[3] + 64] = block[64:]
        for g in range(4):
            upper = tails[(2 + ri) * 4 + g : (2 + ri) * 4 + g + 1]
            lower = tails[ri * 4 + g : ri * 4 + g + 1]
            at = BASES[g] + COUNTS[g]
            gathered_ref[ri, at : at + 1] = jnp.where(lane < 64, upper, lower)
    places = [(beta * 64, beta, 4) for beta in range(4)]
    places += [(256 + v * 64, BASES[1] + v, 2) for v in range(2)]
    places += [(384 + v * 64, BASES[2] + v, 3) for v in range(3)]
    places += [(576, BASES[3], 1)]
    for target, source, stride in places:
        for shift in range(2):
            real, imag = (
                gathered_ref[ri, pl.ds(source + shift, 64, stride=stride), :] for ri in range(2)
            )
            span = slice(shift * 128, shift * 128 + 128)
            for which, values in enumerate((real + imag, real, imag)):
                high, low = halves(values)
                win_high_ref[which, target : target + 64, span] = high
                win_low_ref[which, target : target + 64, span] = low


def power_kernel(
    rows_ref,
    x_ref,
    high_ref,
    low_ref,
    spread_ref,
    out_ref,
    gathered_ref,
    win_high_ref,
    win_low_ref,
    sum_ref,
    lower_ref,
):
    step = pl.program_id(0)

    @pl.when(step == 0)
    def _():
        gather_windows(x_ref, gathered_ref, win_high_ref, win_low_ref)

    @pl.when(step < STEPS)
    def _():
        for pair in range(PAIRS):
            parts = [
                product(
                    (win_high_ref[which], win_low_ref[which]),
                    (high_ref[pair, which], low_ref[pair, which]),
                )
                for which in range(3)
            ]
            real = parts[0] - parts[2]
            imag = parts[0] + parts[1]
            power = real * real + imag * imag
            for at in range(2):
                t = (step * PAIRS + pair) * 2 + at
                span = slice(at * 128, at * 128 + 128)
                sum_ref[pl.ds(t * 256, 256), :] = power[:256, span]
                high, low = halves(power[256:, span])
                lower_ref[t, :, 0:128] = high
                lower_ref[t, :, 128:256] = low

    @pl.when(step >= STEPS)
    def _():
        first = (step - STEPS) * 8
        picks = [[rows_ref[h, first + t] for t in range(8)] for h in range(3)]

        def rows_of(h, at):
            return jnp.concatenate([lower_ref[r, at : at + 64] for r in picks[h]], axis=0)

        for pair in range(2):
            sources = (
                rows_of(0, 320),
                rows_of(1, 64 * pair),
                rows_of(2, 128 + 64 * pair),
                rows_of(2, 192 + 64 * pair),
            )
            spread = jnp.dot(
                jnp.concatenate(sources, axis=1), spread_ref[pair], preferred_element_type=f32
            )
            for u in range(2):
                beta = 2 * pair + u
                for t in range(8):
                    own = sum_ref[pl.ds((first + t) * 256 + beta * 64, 64), :]
                    out_ref[pl.ds(beta * 8 + t, 64, stride=32), :] = (
                        own + spread[t * 64 : t * 64 + 64, u * 128 : u * 128 + 128]
                    )


def swap_blocks(values):
    return lax.all_to_all(values, "freq", split_axis=0, concat_axis=0, tiled=True)


def turn_tables(position):
    m = 128 * jnp.asarray(row_order(), jnp.int32)[:, None] + jnp.arange(128, dtype=jnp.int32)
    tables = []
    for residue in (position, jnp.where(position == 0, 64, position)):
        angles = (m * residue).astype(f32) * (-2.0 * math.pi / SAMPLES)
        tables += [jnp.cos(angles), jnp.sin(angles)]
    return jnp.stack(tables)


def tap_rows(kernels, half_widths):
    offsets = jnp.abs(jnp.arange(2 * MAXHALF + 1, dtype=jnp.int32) - MAXHALF)
    inside = offsets[None, :] <= half_widths[:, None]
    taps = jnp.where(inside[None], kernels, 0.0)
    return jnp.concatenate(
        [taps[:, :, 0:1], jnp.zeros((2, TEMPL, 127), f32), taps[:, :, :0:-1]], axis=2
    ).reshape(2, TEMPL, 1, 256)


def whole(shape):
    return pl.BlockSpec(shape, lambda i: (0,) * len(shape))


def grant(mebibytes):
    return pltpu.CompilerParams(vmem_limit_bytes=mebibytes << 20)


def on_device(series, kernels, half_widths, sub_rows):
    position = lax.axis_index("freq")
    blocks = series.reshape(2, MEMBERS, 4, LANES).transpose(1, 0, 2, 3).reshape(512, LANES)
    arrived = swap_blocks(blocks)
    streams = pl.pallas_call(
        first_kernel,
        out_shape=jax.ShapeDtypeStruct((512, LANES), f32),
        compiler_params=grant(4),
        name="first",
    )(constant_halves(first_matrix()), arrived)
    arrived = swap_blocks(streams)
    outgoing = pl.pallas_call(
        spectrum_kernel,
        in_specs=[pl.BlockSpec()] * 5 + [pl.BlockSpec(memory_space=pltpu.SMEM)],
        out_shape=jax.ShapeDtypeStruct((MEMBERS * ROWS_OUT, LANES), f32),
        scratch_shapes=[pltpu.VMEM((4, 2, 72, 128), f32), pltpu.VMEM((4, 5, 72, 128), f32)],
        compiler_params=grant(12),
        name="spectrum",
    )(
        arrived,
        turn_tables(position),
        constant_halves(second_matrix()),
        jnp.asarray(middle_twiddle()),
        constant_halves(third_matrix()),
        position.reshape(1),
    )
    arrived = swap_blocks(outgoing)
    matrix = jax.ShapeDtypeStruct((TEMPL // 2, 3, 256, 256), bf16)
    tap_block = pl.BlockSpec((1, 3, 256, 256), lambda i: (i, 0, 0, 0))
    tap_high, tap_low = pl.pallas_call(
        taps_kernel,
        grid=(TEMPL // 2,),
        in_specs=[pl.BlockSpec((2, 2, 1, 256), lambda i: (0, i, 0, 0)), whole((64, 64))],
        out_specs=[tap_block, tap_block],
        out_shape=[matrix, matrix],
        compiler_params=grant(58),
        name="taps",
    )(tap_rows(kernels, half_widths), jnp.asarray(flip_matrix()))
    tap_block = pl.BlockSpec(
        (PAIRS, 3, 256, 256), lambda i: (jnp.minimum(i, STEPS - 1), 0, 0, 0)
    )
    summed = pl.pallas_call(
        power_kernel,
        grid=(STEPS + 2,),
        in_specs=[
            pl.BlockSpec(memory_space=pltpu.SMEM),
            whole((MEMBERS * ROWS_OUT, LANES)),
            tap_block,
            tap_block,
            whole((2, 1024, 256)),
        ],
        out_specs=pl.BlockSpec((2048, LANES), lambda i: (jnp.maximum(i - STEPS, 0), 0)),
        out_shape=jax.ShapeDtypeStruct((TEMPL * 256, LANES), f32),
        scratch_shapes=[
            pltpu.VMEM((2, GATHERED, 128), f32),
            pltpu.VMEM((3, WINDOWS, 256), bf16),
            pltpu.VMEM((3, WINDOWS, 256), bf16),
            pltpu.VMEM((TEMPL * 256, 128), f32),
            pltpu.VMEM((TEMPL, 384, 256), bf16),
        ],
        compiler_params=grant(50),
        name="power",
    )(sub_rows, arrived, tap_high, tap_low, jnp.asarray(spread_matrices()))
    return summed.reshape(2, 256, 8, LANES).transpose(0, 2, 1, 3).reshape(TEMPL, 256 * LANES)


def solution(mesh):
    in_specs = (P(("dm", "freq")), P(), P(), P())
    out_specs = P(None, ("dm", "freq"))
    return jax.shard_map(
        on_device, mesh=mesh, in_specs=in_specs, out_specs=out_specs, check_vma=False
    )
```

time: 106 us -> 90.1 us (0.85)
  Pallas kernels: 38.5 us -> 22.3 us
  waiting for transfers between devices: 22 us -> 26.9 us
  local copies, waits for them, and re-layouts: 5.67 us -> 2.97 us
    pallas_call x2, Pallas kernels: 31.5 us -> 18.9 us  [the longest x1 12.6 us: on_device(): pl.pallas_call(power_kernel, grid=(STEPS + 2,), in_specs=[pl.BlockSpec(me...]
    all_to_all x2, waiting for transfers between devices: 22 us -> 26.9 us  [swap_blocks(): lax.all_to_all(values, 'freq', split_axis=0, concat_axis=0, tiled=True)]
    all_to_all x3 -> x1, local copies, waits for them, and re-layouts: 3.14 us -> 0.16 us  [swap_blocks(): lax.all_to_all(values, 'freq', split_axis=0, concat_axis=0, tiled=True)]
    pallas_call x1, Pallas kernels: 5 us -> 2.44 us  [on_device(): pl.pallas_call(spectrum_kernel, in_specs=[pl.BlockSpec()] * 5 + [pl.Block...]
    pallas_call x1, Pallas kernels: 2.05 us -> 0.94 us  [on_device(): pl.pallas_call(first_kernel, out_shape=jax.ShapeDtypeStruct((512, LANES),...]
  transfers between devices with their start and end apart: 2 -> 2, of which waited for: 2 -> 2; matrix products, arithmetic and copies ran while one was open for 3% -> 3% of each run, Pallas kernels for 10% -> 7%
where the time goes in v1:
time: 90.1 us; the launch traced here: 89.5 us
  waiting for transfers between devices  26.9 us (30%)
  blocking collectives  25.8 us (29%)
  Pallas kernels  22.3 us (25%)
  starting transfers between devices  9.55 us (11%)
  local copies, waits for them, and re-layouts  2.97 us (3%)
  other arithmetic  1.82 us (2%)
    all_to_all x2, waiting for transfers between devices, swap_blocks(): lax.all_to_all(values, 'freq', split_axis=0, concat_axis=0, tiled=True)  26.9 us
    all_to_all x1, blocking collectives, swap_blocks(): lax.all_to_all(values, 'freq', split_axis=0, concat_axis=0, tiled=True)  25.8 us
    pallas_call x1, Pallas kernels, on_device(): pl.pallas_call(power_kernel, grid=(STEPS + 2,), in_specs=[pl.BlockSpec(me...  12.6 us
    all_to_all x2, starting transfers between devices, swap_blocks(): lax.all_to_all(values, 'freq', split_axis=0, concat_axis=0, tiled=True)  9.55 us
    pallas_call x1, Pallas kernels, on_device(): pl.pallas_call(taps_kernel, grid=(TEMPL // 2,), in_specs=[pl.BlockSpec((2...  6.36 us
    pallas_call x1, Pallas kernels, on_device(): pl.pallas_call(spectrum_kernel, in_specs=[pl.BlockSpec()] * 5 + [pl.Block...  2.44 us
  transfers between devices with their start and end apart: 2, of which 2 were waited for; matrix products, arithmetic and copies ran while one was open for 3% of the time, Pallas kernels for 7%

profile of v1, /device:TPU:1, one launch (start us, length us, event | category | flops | bytes accessed | tf_op | source)
XLA Modules:
  0.0 89.5 jit_solution(5692180535945375025)
XLA Ops:
  0.0 0.0 copy-start.3
  0.0 0.0 copy-start.2
  0.0 0.0 copy-start
  0.0 1.1 %copy.14 = f32[64,2,4,128]{3,0,2,1:T(8,128)S(1)} copy(f32[64,2,4,128]{3,2,0,1:T(4,128)} %bitcast.19) | data formatting | bytes 524288 | tf_op jit(solution)/shard_map/transpose | solution.py:362
  1.1 0.2 copy.15
  1.3 25.8 %all_to_all.33 = f32[64,8,128]{2,1,0:T(8,128)S(1)} all-to-all(f32[64,8,128]{2,1,0:T(8,128)S(1)} %copy.15), channel_id=1, replica_groups=mesh['dm'=4,'freq'=64] {'freq'}, dimensions={0} | all-to-all | bytes 524288 | tf_op jit(solution)/shard_map/all_to_all | solution.py:331
  27.1 0.8 copy-done.4
  27.9 0.9 %first.1 = f32[512,128]{1,0:T(8,128)} custom-call(bf16[2,128,128]{2,1,0:T(8,128)(2,1)S(1)} %copy-done.4, f32[512,128]{1,0:T(8,128)S(1)} %bitcast.17), custom_call_target="tpu_custom_call" | custom-call | tf_op jit(solution)/shard_map/first/pallas_call | solution.py:364
  28.9 4.8 %all-to-all-start.1 = ((f32[64,8,128]{2,1,0:T(8,128)}), f32[64,8,128]{2,1,0:T(8,128)S(1)}, u32[]{:S(2)}, u32[]{:S(2)}) async-start(f32[64,8,128]{2,1,0:T(8,128)} %bitcast.4), calls=%async_computation.1 | async-start | bytes 524288 | tf_op jit(solution)/shard_map/all_to_all | solution.py:331
  33.7 0.0 copy-start.7
  33.7 0.0 copy-start.6
  33.7 1.7 %fusion.1 = (f32[1,256,128]{2,1,0:T(8,128)S(1)}, f32[1,256,128]{2,1,0:T(8,128)S(1)}, f32[1,256,128]{2,1,0:T(8,128)S(1)}, f32[1,256,128]{2,1,0:T(8,128)S(1)}) fusion(s32[]{:T(128)} %axis_index.12, s32[256]{0:T(256)} %constant.39, s32[]{:T(128)S(6)} %select_n.8), kind=kLoop, calls=%fused_computation.5 | loop fusion | flops 229376 | bytes 525320 | tf_op jit(solution)/shard_map/cos | solution.py:339
  35.4 0.0 copy-start.1
  35.4 0.0 copy-start.5
  35.5 11.3 %all-to-all-done.1 = f32[64,8,128]{2,1,0:T(8,128)S(1)} async-done(((f32[64,8,128]{2,1,0:T(8,128)}), f32[64,8,128]{2,1,0:T(8,128)S(1)}, u32[]{:S(2)}, u32[]{:S(2)}) %all-to-all-start.1) | async-done | bytes 262176 | tf_op jit(solution)/shard_map/all_to_all | solution.py:331
  46.7 0.0 copy-done.3
  46.7 0.0 copy-done.2
  46.7 0.0 copy-done
  46.7 2.4 %spectrum.1 = f32[1536,128]{1,0:T(8,128)} custom-call(f32[512,128]{1,0:T(8,128)S(1)} %bitcast.16, f32[4,256,128]{2,1,0:T(8,128)S(1)} %pad_maximum_fusion.turns_ref, bf16[2,512,512]{2,1,0:T(8,128)(2,1)S(1)} %copy-done, f32[2,256,128]{2,1,0:T(8,128)S(1)} %copy-done.2, bf16[2,144,256]{2,1,0:T(8,128)(2,1)S(1)} %copy-done.3, s32[1]{0:T(128)} %bitcast.6.flag_ref), custom_call_target="tpu_custom_call" | custom-call | tf_op jit(solution)/shard_map/spectrum/pallas_call | solution.py:371
  49.2 4.8 %all-to-all-start.2 = ((f32[64,24,128]{2,1,0:T(8,128)}), f32[64,24,128]{2,1,0:T(8,128)S(1)}, u32[]{:S(2)}, u32[]{:S(2)}) async-start(f32[64,24,128]{2,1,0:T(8,128)} %bitcast.7), calls=%async_computation.2 | async-start | bytes 1572864 | tf_op jit(solution)/shard_map/all_to_all | solution.py:331
  54.0 0.0 copy-done.7
  54.0 0.1 broadcast_compare_fusion
  54.1 0.0 copy-done.6
  54.1 0.1 slice.9
  54.2 0.1 rev.3
  54.2 0.1 pad.1.clone
  54.3 0.6 reshape.175.v_ref
  54.9 6.4 %taps.1 = (bf16[8,3,256,256]{3,2,1,0:T(8,128)(2,1)}, bf16[8,3,256,256]{3,2,1,0:T(8,128)(2,1)}) custom-call(f32[2,16,1,256]{3,2,1,0:T(1,128)} %reshape.175.v_ref, bf16[64,64]{1,0:T(8,128)(2,1)} %constant.37.clone.flip_ref), custom_call_target="tpu_custom_call" | custom-call | tf_op jit(solution)/shard_map/taps/pallas_call | solution.py:389
  61.3 15.7 %all-to-all-done.2 = f32[64,24,128]{2,1,0:T(8,128)S(1)} async-done(((f32[64,24,128]{2,1,0:T(8,128)}), f32[64,24,128]{2,1,0:T(8,128)S(1)}, u32[]{:S(2)}, u32[]{:S(2)}) %all-to-all-start.2) | async-done | bytes 786464 | tf_op jit(solution)/shard_map/all_to_all | solution.py:331
  77.0 0.0 copy-done.1
  77.0 0.0 copy-done.5
  77.0 12.6 %power.1 = f32[4096,128]{1,0:T(8,128)} custom-call(s32[3,16]{1,0:T(4,128)S(1)} %copy-done.5, f32[1536,128]{1,0:T(8,128)S(1)} %bitcast.15, bf16[8,3,256,256]{3,2,1,0:T(8,128)(2,1)} %get-tuple-element.7.high_ref, bf16[8,3,256,256]{3,2,1,0:T(8,128)(2,1)} %get-tuple-element.8.low_ref, bf16[2,1024,256]{2,1,0:T(8,128)(2,1)S(1)} %copy-done.1), custom_call_target="tpu_custom_call" | custom-call | tf_op jit(solution)/shard_map/power/pallas_call | solution.py:401
  (7 shorter events, 0.1 us)
Async XLA Ops:
  0.0 46.7 %copy-start.3 = (bf16[2,144,256]{2,1,0:T(8,128)(2,1)S(1)}, bf16[2,144,256]{2,1,0:T(8,128)(2,1)}, u32[]{:S(2)}) copy-start(bf16[2,144,256]{2,1,0:T(8,128)(2,1)} %constant.36.clone.third_ref) | copy-start | bytes 442372
  0.0 46.7 %copy-start.2 = (f32[2,256,128]{2,1,0:T(8,128)S(1)}, f32[2,256,128]{2,1,0:T(8,128)}, u32[]{:S(2)}) copy-start(f32[2,256,128]{2,1,0:T(8,128)} %constant.35.clone.middle_ref) | copy-start | bytes 786436
  0.0 46.7 %copy-start = (bf16[2,512,512]{2,1,0:T(8,128)(2,1)S(1)}, bf16[2,512,512]{2,1,0:T(8,128)(2,1)}, u32[]{:S(2)}) copy-start(bf16[2,512,512]{2,1,0:T(8,128)(2,1)} %constant.34.clone.second_ref) | copy-start | bytes 3145732
  27.1 0.8 copy-start.4
  28.9 17.9 %all-to-all-start.1 = ((f32[64,8,128]{2,1,0:T(8,128)}), f32[64,8,128]{2,1,0:T(8,128)S(1)}, u32[]{:S(2)}, u32[]{:S(2)}) async-start(f32[64,8,128]{2,1,0:T(8,128)} %bitcast.4), calls=%async_computation.1 | async-start | bytes 524288 | tf_op jit(solution)/shard_map/all_to_all | solution.py:331
  33.7 20.3 %copy-start.7 = (s32[16]{0:T(128)S(1)}, s32[16]{0:T(128)}, u32[]{:S(2)}) copy-start(s32[16]{0:T(128)} %param.13) | copy-start | bytes 196
  33.7 20.4 %copy-start.6 = (f32[2,16,129]{2,1,0:T(8,128)S(1)}, f32[2,16,129]{2,1,0:T(8,128)}, u32[]{:S(2)}) copy-start(f32[2,16,129]{2,1,0:T(8,128)} %param.12) | copy-start | bytes 49540
  35.4 41.6 %copy-start.1 = (bf16[2,1024,256]{2,1,0:T(8,128)(2,1)S(1)}, bf16[2,1024,256]{2,1,0:T(8,128)(2,1)}, u32[]{:S(2)}) copy-start(bf16[2,1024,256]{2,1,0:T(8,128)(2,1)} %constant.38.clone.spread_ref) | copy-start | bytes 3145732
  35.4 41.6 %copy-start.5 = (s32[3,16]{1,0:T(4,128)S(1)}, s32[3,16]{1,0:T(4,128)}, u32[]{:S(2)}) copy-start(s32[3,16]{1,0:T(4,128)} %rows_ref.1) | copy-start | bytes 580
  49.2 27.8 %all-to-all-start.2 = ((f32[64,24,128]{2,1,0:T(8,128)}), f32[64,24,128]{2,1,0:T(8,128)S(1)}, u32[]{:S(2)}, u32[]{:S(2)}) async-start(f32[64,24,128]{2,1,0:T(8,128)} %bitcast.7), calls=%async_computation.2 | async-start | bytes 1572864 | tf_op jit(solution)/shard_map/all_to_all | solution.py:331
